TPU v7x, 32 devices: a whole 2x2x4 slice. The times are simulated.
32 devices in a mesh: row: 8 (over y, x, core), col: 4 (over z).
Axes of the slice: x: 2, y: 2, z: 4, core: 2. Of those that a mesh axis runs over, the one named last changes fastest.
Arguments:
- sub_basis: bfloat16 [32, 768, 768], P(('row', 'col')), may hold values from -0.15625 to 0.15625
- coupling: bfloat16 [32, 2, 768, 768], P(('row', 'col')), may hold values from -0.15625 to 0.15625
- pair_live: int32 [32, 2], P(('row', 'col')), may hold values 0 or 1
- offsets: int32 [32], P(('row', 'col')), may hold values from 0 to 3328
- dual_in: float32 [4, 4096], P('col', 'row'), may hold values from -6 to 6
Outputs:
- dual_out: float32 [4, 4096], P('col', 'row')
Inputs may be any that keep to these rules, and one draw needn't show every extreme that they name: `offsets`: each subdomain's window of 768 multipliers lies inside its block column's vector.
All inputs are finite; a program needn't handle non-finite values. No bound on the sum of `pair_live` on one device may be relied on, other than what follows from the above.
Results may differ from a plain program's by a relative error of at most 0.0085.
Values may be sent and summed in bfloat16 or wider, within the bound.
A program may use at most 64 MiB of HBM per device.

v0:
```python
import jax
import jax.numpy as jnp
from jax import lax
from jax.sharding import PartitionSpec as P


def passed_along(array, axis, by):
    count = lax.axis_size(axis)
    return lax.ppermute(array, axis, [(i, (i + by) % count) for i in range(count)])


def left_apply(matrix, vector):
    return lax.dot_general(
        matrix,
        vector,
        (((1,), (0,)), ((), ())),
        precision=lax.Precision.HIGHEST,
        preferred_element_type=jnp.float32,
    )


def right_apply(vector, matrix):
    return jnp.dot(
        vector, matrix, precision=lax.Precision.HIGHEST, preferred_element_type=jnp.float32
    )


def apply_dual(window, basis, couplings, live):
    projected = left_apply(basis, window)
    inner = projected
    summed = jnp.zeros_like(window)
    for slot, coupling in enumerate(couplings):
        distance = slot + 1
        ahead = passed_along(window, "col", -distance)
        inner = inner + live[slot] * left_apply(coupling, ahead)
        back = live[slot] * right_apply(projected, coupling)
        summed = summed + passed_along(back, "col", distance)
    return summed + right_apply(inner, basis)


def on_device(sub_basis, coupling, pair_live, offsets, dual_in):
    width = sub_basis.shape[2]
    basis = sub_basis[0].astype(jnp.float32)
    couplings = [coupling[0, h].astype(jnp.float32) for h in range(coupling.shape[1])]
    live = pair_live[0].astype(jnp.float32)
    length = dual_in.shape[1] * lax.axis_size("row")
    start = offsets[0]
    piece = dual_in
    for _ in range(2):
        column = lax.all_gather(piece, "row", axis=1, tiled=True)[0]
        window = lax.dynamic_slice_in_dim(column, start, width)
        local = apply_dual(window, basis, couplings, live)
        placed = lax.dynamic_update_slice(jnp.zeros((length,), jnp.float32), local, (start,))
        piece = lax.psum_scatter(placed[None, :], "row", scatter_dimension=1, tiled=True)
    return piece


def solution(mesh):
    return jax.shard_map(
        on_device,
        mesh=mesh,
        in_specs=(
            P(("row", "col"), None, None),
            P(("row", "col"), None, None, None),
            P(("row", "col"), None),
            P(("row", "col")),
            P("col", "row"),
        ),
        out_specs=P("col", "row"),
        check_vma=False,
    )
```

profile of v0, /device:TPU:0, one launch (start us, length us, event | category | flops | bytes accessed | tf_op | source)
XLA Modules:
  0.0 154.4 jit_solution(13610832899957684372)
XLA Ops:
  7.3 10.5 %all_gather.6 = f32[1,4096]{1,0:T(1,128)S(1)} all-gather(f32[1,512]{1,0:T(1,128)} %param.9), channel_id=1, replica_groups=mesh['row'=8,'col'=4] {'row'}, dimensions={1}, use_global_device_ids=true | all-gather | bytes 18432 | tf_op jit(solution)/shard_map/all_gather | solution.py:50
  17.9 3.7 %collective-permute-start.2 = (f32[768]{0:T(1024)S(1)}, f32[768]{0:T(1024)S(1)}, u32[]{:S(2)}, u32[]{:S(2)}) collective-permute-start(f32[768]{0:T(1024)S(1)} %dynamic-slice_reduce_fusion.1), channel_id=1, source_target_pairs={{0,3},{1,0},{2,1},{3,2},{4,7},{5,4},{6,5},{7,6},{8,11},{9,8},{10,9... | collective-permute-start | bytes 9224 | tf_op jit(solution)/shard_map/ppermute | solution.py:9
  21.5 1.1 fusion.73
  23.2 1.9 %fusion.30 = f32[768]{0:T(1024)S(1)} fusion(bf16[1,2,768,768]{3,2,1,0:T(8,128)(2,1)} %param.6, f32[1,768]{1,0:T(1,128)S(1)} %get-tuple-element.8), kind=kOutput, calls=%fused_computation.26 | convolution fusion | flops 7077888 | bytes 1185792 | tf_op jit(solution)/shard_map/dot_general | solution.py:23
  25.8 1.1 collective-permute-start
  28.0 2.0 %collective-permute-start.1 = (f32[768]{0:T(1024)S(1)}, f32[768]{0:T(1024)S(1)}, u32[]{:S(2)}, u32[]{:S(2)}) collective-permute-start(f32[768]{0:T(1024)S(1)} %broadcast_multiply_fusion.1), channel_id=1, source_target_pairs={{0,2},{1,3},{2,0},{3,1},{4,6},{5,7},{6,4},{7,5},{8,10},{9,11},{10,... | collective-permute-start | bytes 9224 | tf_op jit(solution)/shard_map/ppermute | solution.py:9
  30.0 1.1 fusion.33
  31.1 1.1 fusion.45
  32.2 1.2 multiply_add_fusion.1
  34.6 0.8 dynamic_update_slice.8
  35.5 2.0 %copy.6 = f32[1,4096]{0,1:T(8,128)} copy(f32[1,4096]{1,0:T(1,128)S(1)} %dynamic_update_slice.8) | data formatting | bytes 32768
  37.5 41.0 %reduce-scatter.7.cloned.1.call-done = f32[512,1]{1,0:T(8,128)} async-done(((f32[4096,1]{1,0:T(8,128)}), f32[512,1]{1,0:T(8,128)}) %reduce-scatter.7.cloned.1.call-update) | async-done | bytes 2064
  78.6 1.1 copy.7
  79.6 8.8 %all_gather.7 = f32[1,4096]{1,0:T(1,128)S(1)} all-gather(f32[1,512]{1,0:T(1,128)S(1)} %copy.7), channel_id=1, replica_groups=mesh['row'=8,'col'=4] {'row'}, dimensions={1}, use_global_device_ids=true | all-gather | bytes 18432 | tf_op jit(solution)/shard_map/all_gather | solution.py:50
  88.6 3.4 %collective-permute-start.6 = (f32[768]{0:T(1024)S(1)}, f32[768]{0:T(1024)S(1)}, u32[]{:S(2)}, u32[]{:S(2)}) collective-permute-start(f32[768]{0:T(1024)S(1)} %dynamic-slice_reduce_fusion), channel_id=1, source_target_pairs={{0,3},{1,0},{2,1},{3,2},{4,7},{5,4},{6,5},{7,6},{8,11},{9,8},{10,9... | collective-permute-start | bytes 9224 | tf_op jit(solution)/shard_map/ppermute | solution.py:9
  91.9 1.1 fusion.74
  94.9 1.1 collective-permute-start.4
  96.6 1.9 %collective-permute-start.5 = (f32[768]{0:T(1024)S(1)}, f32[768]{0:T(1024)S(1)}, u32[]{:S(2)}, u32[]{:S(2)}) collective-permute-start(f32[768]{0:T(1024)S(1)} %broadcast_multiply_fusion), channel_id=1, source_target_pairs={{0,2},{1,3},{2,0},{3,1},{4,6},{5,7},{6,4},{7,5},{8,10},{9,11},{10,... | collective-permute-start | bytes 9224 | tf_op jit(solution)/shard_map/ppermute | solution.py:9
  98.5 1.1 fusion.39
  99.6 1.1 fusion.51
  100.7 1.2 multiply_add_fusion
  102.8 2.0 %copy.8 = f32[1,4096]{0,1:T(8,128)} copy(f32[1,4096]{1,0:T(1,128)S(1)} %dynamic_update_slice.9) | data formatting | bytes 32768
  104.8 41.1 %reduce-scatter.9.cloned.1.call-done = f32[512,1]{1,0:T(8,128)} async-done(((f32[4096,1]{1,0:T(8,128)}), f32[512,1]{1,0:T(8,128)}) %reduce-scatter.9.cloned.1.call-update) | async-done | bytes 2064
  145.9 1.6 %copy.9 = f32[1,512]{1,0:T(1,128)} copy(f32[1,512]{0,1:T(8,128)} %bitcast.90) | data formatting | bytes 4096
  (46 shorter events, 7.1 us)
Async XLA Ops:
  6.5 15.0 %copy-start = (bf16[1,768,768]{2,1,0:T(8,128)(2,1)S(1)}, bf16[1,768,768]{2,1,0:T(8,128)(2,1)}, u32[]{:S(2)}) copy-start(bf16[1,768,768]{2,1,0:T(8,128)(2,1)} %param.5) | copy-start | bytes 3538948
  6.5 72.0 %reduce-scatter.7.cloned.1.call-start = ((), (), s32[]{:S(2)}) async-start(), calls=%async_computation.2 | async-start | bytes 2359296
  17.8 4.9 %copy-start.2 = (s32[1,2]{1,0:T(1,128)S(1)}, s32[1,2]{1,0:T(1,128)}, u32[]{:S(2)}) copy-start(s32[1,2]{1,0:T(1,128)} %param.7) | copy-start | bytes 28
  17.9 9.0 %copy-start.1 = (bf16[1,2,768,768]{3,2,1,0:T(8,128)(2,1)S(1)}, bf16[1,2,768,768]{3,2,1,0:T(8,128)(2,1)}, u32[]{:S(2)}) copy-start(bf16[1,2,768,768]{3,2,1,0:T(8,128)(2,1)} %param.6) | copy-start | bytes 7077892
  17.9 12.1 %collective-permute-start.2 = (f32[768]{0:T(1024)S(1)}, f32[768]{0:T(1024)S(1)}, u32[]{:S(2)}, u32[]{:S(2)}) collective-permute-start(f32[768]{0:T(1024)S(1)} %dynamic-slice_reduce_fusion.1), channel_id=1, source_target_pairs={{0,3},{1,0},{2,1},{3,2},{4,7},{5,4},{6,5},{7,6},{8,11},{9,8},{10,9... | collective-permute-start | bytes 9224 | tf_op jit(solution)/shard_map/ppermute | solution.py:9
  21.5 9.5 %collective-permute-start.3 = (f32[768]{0:T(1024)S(1)}, f32[768]{0:T(1024)S(1)}, u32[]{:S(2)}, u32[]{:S(2)}) collective-permute-start(f32[768]{0:T(1024)S(1)} %dynamic-slice_reduce_fusion.1), channel_id=1, source_target_pairs={{0,2},{1,3},{2,0},{3,1},{4,6},{5,7},{6,4},{7,5},{8,10},{9,11},{10,... | collective-permute-start | bytes 9224 | tf_op jit(solution)/shard_map/ppermute | solution.py:9
  25.8 8.2 %collective-permute-start = (f32[768]{0:T(1024)S(1)}, f32[768]{0:T(1024)S(1)}, u32[]{:S(2)}, u32[]{:S(2)}) collective-permute-start(f32[768]{0:T(1024)S(1)} %broadcast_multiply_fusion.3), channel_id=1, source_target_pairs={{0,1},{1,2},{2,3},{3,0},{4,5},{5,6},{6,7},{7,4},{8,9},{9,10},{10,1... | collective-permute-start | bytes 9224 | tf_op jit(solution)/shard_map/ppermute | solution.py:9
  28.0 6.0 %collective-permute-start.1 = (f32[768]{0:T(1024)S(1)}, f32[768]{0:T(1024)S(1)}, u32[]{:S(2)}, u32[]{:S(2)}) collective-permute-start(f32[768]{0:T(1024)S(1)} %broadcast_multiply_fusion.1), channel_id=1, source_target_pairs={{0,2},{1,3},{2,0},{3,1},{4,6},{5,7},{6,4},{7,5},{8,10},{9,11},{10,... | collective-permute-start | bytes 9224 | tf_op jit(solution)/shard_map/ppermute | solution.py:9
  37.5 108.4 %reduce-scatter.9.cloned.1.call-start = ((), (), s32[]{:S(2)}) async-start(), calls=%async_computation.3 | async-start | bytes 2359296
  88.6 10.0 %collective-permute-start.6 = (f32[768]{0:T(1024)S(1)}, f32[768]{0:T(1024)S(1)}, u32[]{:S(2)}, u32[]{:S(2)}) collective-permute-start(f32[768]{0:T(1024)S(1)} %dynamic-slice_reduce_fusion), channel_id=1, source_target_pairs={{0,3},{1,0},{2,1},{3,2},{4,7},{5,4},{6,5},{7,6},{8,11},{9,8},{10,9... | collective-permute-start | bytes 9224 | tf_op jit(solution)/shard_map/ppermute | solution.py:9
  91.9 7.7 %collective-permute-start.7 = (f32[768]{0:T(1024)S(1)}, f32[768]{0:T(1024)S(1)}, u32[]{:S(2)}, u32[]{:S(2)}) collective-permute-start(f32[768]{0:T(1024)S(1)} %dynamic-slice_reduce_fusion), channel_id=1, source_target_pairs={{0,2},{1,3},{2,0},{3,1},{4,6},{5,7},{6,4},{7,5},{8,10},{9,11},{10,... | collective-permute-start | bytes 9224 | tf_op jit(solution)/shard_map/ppermute | solution.py:9
  94.9 7.6 %collective-permute-start.4 = (f32[768]{0:T(1024)S(1)}, f32[768]{0:T(1024)S(1)}, u32[]{:S(2)}, u32[]{:S(2)}) collective-permute-start(f32[768]{0:T(1024)S(1)} %broadcast_multiply_fusion.2), channel_id=1, source_target_pairs={{0,1},{1,2},{2,3},{3,0},{4,5},{5,6},{6,7},{7,4},{8,9},{9,10},{10,1... | collective-permute-start | bytes 9224 | tf_op jit(solution)/shard_map/ppermute | solution.py:9
  96.6 5.9 %collective-permute-start.5 = (f32[768]{0:T(1024)S(1)}, f32[768]{0:T(1024)S(1)}, u32[]{:S(2)}, u32[]{:S(2)}) collective-permute-start(f32[768]{0:T(1024)S(1)} %broadcast_multiply_fusion), channel_id=1, source_target_pairs={{0,2},{1,3},{2,0},{3,1},{4,6},{5,7},{6,4},{7,5},{8,10},{9,11},{10,... | collective-permute-start | bytes 9224 | tf_op jit(solution)/shard_map/ppermute | solution.py:9
Sparse Core Ops, SparseCore 0:
  37.6 40.9 reduce-scatter.6
  104.9 40.9 reduce-scatter.8
where the time goes:
time: 155 us; the launch traced here: 154 us
  waiting for transfers between devices  82.2 us (53%)
  blocking collectives  19.3 us (12%)
  between operations  14.5 us (9%)
  starting transfers between devices  13.2 us (9%)
  matrix products  11.3 us (7%)
  local copies, waits for them, and re-layouts  9.11 us (6%)
  other arithmetic  4.85 us (3%)
    unnamed x4, waiting for transfers between devices  82.2 us
    all_gather x2, blocking collectives, on_device(): column = lax.all_gather(piece, 'row', axis=1, tiled=True)[0]  19.3 us
    ppermute x8, starting transfers between devices, passed_along(): lax.ppermute(array, axis, [(i, (i + by) % count) for i in range(count)])  13.1 us
    unnamed x10, local copies, waits for them, and re-layouts  6.72 us
    dot_general x6, matrix products, left_apply(): lax.dot_general(matrix, vector, (((1,), (0,)), ((), ())), precision=lax.P...  6.42 us
    dot_general x6, matrix products, right_apply(): jnp.dot(vector, matrix, precision=lax.Precision.HIGHEST, preferred_elemen...  4.84 us
  transfers between devices with their start and end apart: 10, of which 2 were waited for; matrix products, arithmetic and copies ran while one was open for 11% of the time, Pallas kernels for 0%

commit v1 on v0

--- a/solution.py
+++ b/solution.py
@@ -2,6 +2,19 @@
 import jax.numpy as jnp
 from jax import lax
 from jax.sharding import PartitionSpec as P
+
+
+def ring_gather(x, axis, dim):
+    ways = lax.axis_size(axis)
+    up = [(d, (d + 1) % ways) for d in range(ways)]
+    down = [(d, (d - 1) % ways) for d in range(ways)]
+    earlier, later = ([x], [x])
+    for _ in range(ways // 2):
+        earlier.append(lax.ppermute(earlier[-1], axis, up))
+    for _ in range((ways - 1) // 2):
+        later.append(lax.ppermute(later[-1], axis, down))
+    line = jnp.concatenate([*earlier[::-1], *later[1:]], axis=dim)
+    return jnp.roll(line, (lax.axis_index(axis) - ways // 2) * x.shape[dim], axis=dim)
 
 
 def passed_along(array, axis, by):
@@ -47,7 +60,7 @@
     start = offsets[0]
     piece = dual_in
     for _ in range(2):
-        column = lax.all_gather(piece, "row", axis=1, tiled=True)[0]
+        column = ring_gather(piece, "row", 1)[0]
         window = lax.dynamic_slice_in_dim(column, start, width)
         local = apply_dual(window, basis, couplings, live)
         placed = lax.dynamic_update_slice(jnp.zeros((length,), jnp.float32), local, (start,))

time: 155 us -> 168 us (1.084)
  blocking collectives: 19.3 us -> 0 us
  starting transfers between devices: 13.2 us -> 30.3 us
  waiting for transfers between devices: 82.2 us -> 96.3 us
    all_gather x2 -> x0, blocking collectives: 19.3 us -> none  [on_device(): column = lax.all_gather(piece, 'row', axis=1, tiled=True)[0]]
    ppermute x0 -> x14, starting transfers between devices: none -> 16.3 us  [the longest x6 15.8 us: ring_gather(): later.append(lax.ppermute(later[-1], axis, down))]
    ppermute x0 -> x14, waiting for transfers between devices: none -> 14 us  [the longest x8 13.9 us: ring_gather(): earlier.append(lax.ppermute(earlier[-1], axis, up))]
    unnamed x10 -> x22, local copies, waits for them, and re-layouts: 6.72 us -> 7.49 us
  transfers between devices with their start and end apart: 10 -> 24, of which waited for: 2 -> 10; matrix products, arithmetic and copies ran while one was open for 11% -> 10% of each run, Pallas kernels for 0% -> 0%
where the time goes in v1:
time: 168 us
  waiting for transfers between devices  96.3 us (57%)
  starting transfers between devices  30.3 us (18%)
  between operations  14.4 us (9%)
  matrix products  11.3 us (7%)
  local copies, waits for them, and re-layouts  9.74 us (6%)
  other arithmetic  5.62 us (3%)
    unnamed x4, waiting for transfers between devices  82.3 us
    ppermute x6, starting transfers between devices, ring_gather(): later.append(lax.ppermute(later[-1], axis, down))  15.8 us
    ppermute x8, starting transfers between devices, passed_along(): lax.ppermute(array, axis, [(i, (i + by) % count) for i in range(count)])  13.9 us
    ppermute x8, waiting for transfers between devices, ring_gather(): earlier.append(lax.ppermute(earlier[-1], axis, up))  13.9 us
    unnamed x22, local copies, waits for them, and re-layouts  7.49 us
    dot_general x6, matrix products, left_apply(): lax.dot_general(matrix, vector, (((1,), (0,)), ((), ())), precision=lax.P...  6.45 us
    dot_general x6, matrix products, right_apply(): jnp.dot(vector, matrix, precision=lax.Precision.HIGHEST, preferred_elemen...  4.84 us
  transfers between devices with their start and end apart: 24, of which 10 were waited for; matrix products, arithmetic and copies ran while one was open for 10% of the time, Pallas kernels for 0%

profile of v1, /device:TPU:0, one launch (start us, length us, event | category | flops | bytes accessed | tf_op | source)
XLA Modules:
  0.0 167.7 jit_solution(6566768334228420817)
XLA Ops:
  7.0 4.4 %collective-permute-done = f32[1,512]{1,0:T(1,128)S(1)} collective-permute-done((f32[1,512]{1,0:T(1,128)}, f32[1,512]{1,0:T(1,128)S(1)}, u32[]{:S(2)}, u32[]{:S(2)}) %collective-permute-start) | collective-permute-done | bytes 2080 | tf_op jit(solution)/shard_map/ppermute | solution.py:13
  11.4 2.6 %collective-permute-start.4 = (f32[1,512]{1,0:T(1,128)}, f32[1,512]{1,0:T(1,128)S(1)}, u32[]{:S(2)}, u32[]{:S(2)}) collective-permute-start(f32[1,512]{1,0:T(1,128)} %param.11), channel_id=1, source_target_pairs={{0,28},{4,0},{8,4},{12,8},{16,12},{20,16},{24,20},{28,24},{1,29},{... | collective-permute-start | bytes 6152 | tf_op jit(solution)/shard_map/ppermute | solution.py:15
  15.9 2.6 %collective-permute-start.5 = (f32[1,512]{1,0:T(1,128)S(1)}, f32[1,512]{1,0:T(1,128)S(1)}, u32[]{:S(2)}, u32[]{:S(2)}) collective-permute-start(f32[1,512]{1,0:T(1,128)S(1)} %collective-permute-done.4), channel_id=1, source_target_pairs={{0,28},{4,0},{8,4},{12,8},{16,12},{20,16},{24,20},{28,24},{1,29},{... | collective-permute-start | bytes 6152 | tf_op jit(solution)/shard_map/ppermute | solution.py:15
  19.8 2.7 %collective-permute-start.6 = (f32[1,512]{1,0:T(1,128)S(1)}, f32[1,512]{1,0:T(1,128)S(1)}, u32[]{:S(2)}, u32[]{:S(2)}) collective-permute-start(f32[1,512]{1,0:T(1,128)S(1)} %collective-permute-done.5), channel_id=1, source_target_pairs={{0,28},{4,0},{8,4},{12,8},{16,12},{20,16},{24,20},{28,24},{1,29},{... | collective-permute-start | bytes 6152 | tf_op jit(solution)/shard_map/ppermute | solution.py:15
  24.0 4.4 %collective-permute-start.9 = (f32[768]{0:T(1024)S(1)}, f32[768]{0:T(1024)S(1)}, u32[]{:S(2)}, u32[]{:S(2)}) collective-permute-start(f32[768]{0:T(1024)S(1)} %fusion.70), channel_id=1, source_target_pairs={{0,3},{1,0},{2,1},{3,2},{4,7},{5,4},{6,5},{7,6},{8,11},{9,8},{10,9... | collective-permute-start | bytes 9224 | tf_op jit(solution)/shard_map/ppermute | solution.py:22
  29.5 1.9 %fusion.30 = f32[768]{0:T(1024)S(1)} fusion(bf16[1,2,768,768]{3,2,1,0:T(8,128)(2,1)} %param.8, f32[1,768]{1,0:T(1,128)S(1)} %get-tuple-element.9), kind=kOutput, calls=%fused_computation.26 | convolution fusion | flops 7077888 | bytes 1185792 | tf_op jit(solution)/shard_map/dot_general | solution.py:36
  34.2 2.0 %collective-permute-start.8 = (f32[768]{0:T(1024)S(1)}, f32[768]{0:T(1024)S(1)}, u32[]{:S(2)}, u32[]{:S(2)}) collective-permute-start(f32[768]{0:T(1024)S(1)} %broadcast_multiply_fusion.1), channel_id=1, source_target_pairs={{0,2},{1,3},{2,0},{3,1},{4,6},{5,7},{6,4},{7,5},{8,10},{9,11},{10,... | collective-permute-start | bytes 9224 | tf_op jit(solution)/shard_map/ppermute | solution.py:22
  38.4 1.2 multiply_add_fusion.1
  41.7 2.0 %copy.6 = f32[1,4096]{0,1:T(8,128)} copy(f32[1,4096]{1,0:T(1,128)S(1)} %dynamic_update_slice.8) | data formatting | bytes 32768
  43.8 41.1 %reduce-scatter.7.cloned.1.call-done = f32[512,1]{1,0:T(8,128)} async-done(((f32[4096,1]{1,0:T(8,128)}), f32[512,1]{1,0:T(8,128)}) %reduce-scatter.7.cloned.1.call-update) | async-done | bytes 2064
  86.0 3.9 %collective-permute-done.11 = f32[1,512]{1,0:T(1,128)S(1)} collective-permute-done((f32[1,512]{1,0:T(1,128)S(1)}, f32[1,512]{1,0:T(1,128)S(1)}, u32[]{:S(2)}, u32[]{:S(2)}) %collective-permute-start.11) | collective-permute-done | bytes 2080 | tf_op jit(solution)/shard_map/ppermute | solution.py:13
  89.9 2.6 %collective-permute-start.15 = (f32[1,512]{1,0:T(1,128)S(1)}, f32[1,512]{1,0:T(1,128)S(1)}, u32[]{:S(2)}, u32[]{:S(2)}) collective-permute-start(f32[1,512]{1,0:T(1,128)S(1)} %copy.7), channel_id=1, source_target_pairs={{0,28},{4,0},{8,4},{12,8},{16,12},{20,16},{24,20},{28,24},{1,29},{... | collective-permute-start | bytes 6152 | tf_op jit(solution)/shard_map/ppermute | solution.py:15
  92.5 1.3 collective-permute-done.12
  93.9 2.6 %collective-permute-start.16 = (f32[1,512]{1,0:T(1,128)S(1)}, f32[1,512]{1,0:T(1,128)S(1)}, u32[]{:S(2)}, u32[]{:S(2)}) collective-permute-start(f32[1,512]{1,0:T(1,128)S(1)} %collective-permute-done.15), channel_id=1, source_target_pairs={{0,28},{4,0},{8,4},{12,8},{16,12},{20,16},{24,20},{28,24},{1,29},{... | collective-permute-start | bytes 6152 | tf_op jit(solution)/shard_map/ppermute | solution.py:15
  96.5 1.3 collective-permute-done.13
  97.8 2.6 %collective-permute-start.17 = (f32[1,512]{1,0:T(1,128)S(1)}, f32[1,512]{1,0:T(1,128)S(1)}, u32[]{:S(2)}, u32[]{:S(2)}) collective-permute-start(f32[1,512]{1,0:T(1,128)S(1)} %collective-permute-done.16), channel_id=1, source_target_pairs={{0,28},{4,0},{8,4},{12,8},{16,12},{20,16},{24,20},{28,24},{1,29},{... | collective-permute-start | bytes 6152 | tf_op jit(solution)/shard_map/ppermute | solution.py:15
  100.4 1.3 collective-permute-done.14
  102.9 3.4 %collective-permute-start.20 = (f32[768]{0:T(1024)S(1)}, f32[768]{0:T(1024)S(1)}, u32[]{:S(2)}, u32[]{:S(2)}) collective-permute-start(f32[768]{0:T(1024)S(1)} %fusion.72), channel_id=1, source_target_pairs={{0,3},{1,0},{2,1},{3,2},{4,7},{5,4},{6,5},{7,6},{8,11},{9,8},{10,9... | collective-permute-start | bytes 9224 | tf_op jit(solution)/shard_map/ppermute | solution.py:22
  108.1 1.2 collective-permute-start.18
  109.9 1.9 %collective-permute-start.19 = (f32[768]{0:T(1024)S(1)}, f32[768]{0:T(1024)S(1)}, u32[]{:S(2)}, u32[]{:S(2)}) collective-permute-start(f32[768]{0:T(1024)S(1)} %broadcast_multiply_fusion), channel_id=1, source_target_pairs={{0,2},{1,3},{2,0},{3,1},{4,6},{5,7},{6,4},{7,5},{8,10},{9,11},{10,... | collective-permute-start | bytes 9224 | tf_op jit(solution)/shard_map/ppermute | solution.py:22
  114.0 1.2 multiply_add_fusion
  116.0 2.0 %copy.8 = f32[1,4096]{0,1:T(8,128)} copy(f32[1,4096]{1,0:T(1,128)S(1)} %dynamic_update_slice.9) | data formatting | bytes 32768
  118.0 41.2 %reduce-scatter.9.cloned.1.call-done = f32[512,1]{1,0:T(8,128)} async-done(((f32[4096,1]{1,0:T(8,128)}), f32[512,1]{1,0:T(8,128)}) %reduce-scatter.9.cloned.1.call-update) | async-done | bytes 2064
  159.2 1.6 copy.9
  (86 shorter events, 20.4 us)
Async XLA Ops:
  6.5 78.4 %reduce-scatter.7.cloned.1.call-start = ((), (), s32[]{:S(2)}) async-start(), calls=%async_computation.2 | async-start | bytes 2359296
  6.5 4.8 %collective-permute-start = (f32[1,512]{1,0:T(1,128)}, f32[1,512]{1,0:T(1,128)S(1)}, u32[]{:S(2)}, u32[]{:S(2)}) collective-permute-start(f32[1,512]{1,0:T(1,128)} %param.11), channel_id=1, source_target_pairs={{0,4},{4,8},{8,12},{12,16},{16,20},{20,24},{24,28},{28,0},{1,5},{5... | collective-permute-start | bytes 6152 | tf_op jit(solution)/shard_map/ppermute | solution.py:13
  11.4 3.9 %collective-permute-start.1 = (f32[1,512]{1,0:T(1,128)S(1)}, f32[1,512]{1,0:T(1,128)S(1)}, u32[]{:S(2)}, u32[]{:S(2)}) collective-permute-start(f32[1,512]{1,0:T(1,128)S(1)} %collective-permute-done), channel_id=1, source_target_pairs={{0,4},{4,8},{8,12},{12,16},{16,20},{20,24},{24,28},{28,0},{1,5},{5... | collective-permute-start | bytes 6152 | tf_op jit(solution)/shard_map/ppermute | solution.py:13
  11.4 4.5 %collective-permute-start.4 = (f32[1,512]{1,0:T(1,128)}, f32[1,512]{1,0:T(1,128)S(1)}, u32[]{:S(2)}, u32[]{:S(2)}) collective-permute-start(f32[1,512]{1,0:T(1,128)} %param.11), channel_id=1, source_target_pairs={{0,28},{4,0},{8,4},{12,8},{16,12},{20,16},{24,20},{28,24},{1,29},{... | collective-permute-start | bytes 6152 | tf_op jit(solution)/shard_map/ppermute | solution.py:15
  15.3 3.9 %collective-permute-start.2 = (f32[1,512]{1,0:T(1,128)S(1)}, f32[1,512]{1,0:T(1,128)S(1)}, u32[]{:S(2)}, u32[]{:S(2)}) collective-permute-start(f32[1,512]{1,0:T(1,128)S(1)} %collective-permute-done.1), channel_id=1, source_target_pairs={{0,4},{4,8},{8,12},{12,16},{16,20},{20,24},{24,28},{28,0},{1,5},{5... | collective-permute-start | bytes 6152 | tf_op jit(solution)/shard_map/ppermute | solution.py:13
  15.9 4.0 %collective-permute-start.5 = (f32[1,512]{1,0:T(1,128)S(1)}, f32[1,512]{1,0:T(1,128)S(1)}, u32[]{:S(2)}, u32[]{:S(2)}) collective-permute-start(f32[1,512]{1,0:T(1,128)S(1)} %collective-permute-done.4), channel_id=1, source_target_pairs={{0,28},{4,0},{8,4},{12,8},{16,12},{20,16},{24,20},{28,24},{1,29},{... | collective-permute-start | bytes 6152 | tf_op jit(solution)/shard_map/ppermute | solution.py:15
  19.2 3.9 %collective-permute-start.3 = (f32[1,512]{1,0:T(1,128)S(1)}, f32[1,512]{1,0:T(1,128)S(1)}, u32[]{:S(2)}, u32[]{:S(2)}) collective-permute-start(f32[1,512]{1,0:T(1,128)S(1)} %collective-permute-done.2), channel_id=1, source_target_pairs={{0,4},{4,8},{8,12},{12,16},{16,20},{20,24},{24,28},{28,0},{1,5},{5... | collective-permute-start | bytes 6152 | tf_op jit(solution)/shard_map/ppermute | solution.py:13
  19.8 4.0 %collective-permute-start.6 = (f32[1,512]{1,0:T(1,128)S(1)}, f32[1,512]{1,0:T(1,128)S(1)}, u32[]{:S(2)}, u32[]{:S(2)}) collective-permute-start(f32[1,512]{1,0:T(1,128)S(1)} %collective-permute-done.5), channel_id=1, source_target_pairs={{0,28},{4,0},{8,4},{12,8},{16,12},{20,16},{24,20},{28,24},{1,29},{... | collective-permute-start | bytes 6152 | tf_op jit(solution)/shard_map/ppermute | solution.py:15
  24.0 12.3 %collective-permute-start.9 = (f32[768]{0:T(1024)S(1)}, f32[768]{0:T(1024)S(1)}, u32[]{:S(2)}, u32[]{:S(2)}) collective-permute-start(f32[768]{0:T(1024)S(1)} %fusion.70), channel_id=1, source_target_pairs={{0,3},{1,0},{2,1},{3,2},{4,7},{5,4},{6,5},{7,6},{8,11},{9,8},{10,9... | collective-permute-start | bytes 9224 | tf_op jit(solution)/shard_map/ppermute | solution.py:22
  28.4 8.9 %collective-permute-start.10 = (f32[768]{0:T(1024)S(1)}, f32[768]{0:T(1024)S(1)}, u32[]{:S(2)}, u32[]{:S(2)}) collective-permute-start(f32[768]{0:T(1024)S(1)} %fusion.70), channel_id=1, source_target_pairs={{0,2},{1,3},{2,0},{3,1},{4,6},{5,7},{6,4},{7,5},{8,10},{9,11},{10,... | collective-permute-start | bytes 9224 | tf_op jit(solution)/shard_map/ppermute | solution.py:22
  32.5 7.7 %collective-permute-start.7 = (f32[768]{0:T(1024)S(1)}, f32[768]{0:T(1024)S(1)}, u32[]{:S(2)}, u32[]{:S(2)}) collective-permute-start(f32[768]{0:T(1024)S(1)} %broadcast_multiply_fusion.3), channel_id=1, source_target_pairs={{0,1},{1,2},{2,3},{3,0},{4,5},{5,6},{6,7},{7,4},{8,9},{9,10},{10,1... | collective-permute-start | bytes 9224 | tf_op jit(solution)/shard_map/ppermute | solution.py:22
  34.2 6.0 %collective-permute-start.8 = (f32[768]{0:T(1024)S(1)}, f32[768]{0:T(1024)S(1)}, u32[]{:S(2)}, u32[]{:S(2)}) collective-permute-start(f32[768]{0:T(1024)S(1)} %broadcast_multiply_fusion.1), channel_id=1, source_target_pairs={{0,2},{1,3},{2,0},{3,1},{4,6},{5,7},{6,4},{7,5},{8,10},{9,11},{10,... | collective-permute-start | bytes 9224 | tf_op jit(solution)/shard_map/ppermute | solution.py:22
  43.7 115.5 %reduce-scatter.9.cloned.1.call-start = ((), (), s32[]{:S(2)}) async-start(), calls=%async_computation.3 | async-start | bytes 2359296
  86.0 3.9 %collective-permute-start.11 = (f32[1,512]{1,0:T(1,128)S(1)}, f32[1,512]{1,0:T(1,128)S(1)}, u32[]{:S(2)}, u32[]{:S(2)}) collective-permute-start(f32[1,512]{1,0:T(1,128)S(1)} %copy.7), channel_id=1, source_target_pairs={{0,4},{4,8},{8,12},{12,16},{16,20},{20,24},{24,28},{28,0},{1,5},{5... | collective-permute-start | bytes 6152 | tf_op jit(solution)/shard_map/ppermute | solution.py:13
  89.9 3.9 %collective-permute-start.12 = (f32[1,512]{1,0:T(1,128)S(1)}, f32[1,512]{1,0:T(1,128)S(1)}, u32[]{:S(2)}, u32[]{:S(2)}) collective-permute-start(f32[1,512]{1,0:T(1,128)S(1)} %collective-permute-done.11), channel_id=1, source_target_pairs={{0,4},{4,8},{8,12},{12,16},{16,20},{20,24},{24,28},{28,0},{1,5},{5... | collective-permute-start | bytes 6152 | tf_op jit(solution)/shard_map/ppermute | solution.py:13
  89.9 4.0 %collective-permute-start.15 = (f32[1,512]{1,0:T(1,128)S(1)}, f32[1,512]{1,0:T(1,128)S(1)}, u32[]{:S(2)}, u32[]{:S(2)}) collective-permute-start(f32[1,512]{1,0:T(1,128)S(1)} %copy.7), channel_id=1, source_target_pairs={{0,28},{4,0},{8,4},{12,8},{16,12},{20,16},{24,20},{28,24},{1,29},{... | collective-permute-start | bytes 6152 | tf_op jit(solution)/shard_map/ppermute | solution.py:15
  93.8 3.9 %collective-permute-start.13 = (f32[1,512]{1,0:T(1,128)S(1)}, f32[1,512]{1,0:T(1,128)S(1)}, u32[]{:S(2)}, u32[]{:S(2)}) collective-permute-start(f32[1,512]{1,0:T(1,128)S(1)} %collective-permute-done.12), channel_id=1, source_target_pairs={{0,4},{4,8},{8,12},{12,16},{16,20},{20,24},{24,28},{28,0},{1,5},{5... | collective-permute-start | bytes 6152 | tf_op jit(solution)/shard_map/ppermute | solution.py:13
  93.9 3.9 %collective-permute-start.16 = (f32[1,512]{1,0:T(1,128)S(1)}, f32[1,512]{1,0:T(1,128)S(1)}, u32[]{:S(2)}, u32[]{:S(2)}) collective-permute-start(f32[1,512]{1,0:T(1,128)S(1)} %collective-permute-done.15), channel_id=1, source_target_pairs={{0,28},{4,0},{8,4},{12,8},{16,12},{20,16},{24,20},{28,24},{1,29},{... | collective-permute-start | bytes 6152 | tf_op jit(solution)/shard_map/ppermute | solution.py:15
  97.7 3.9 %collective-permute-start.14 = (f32[1,512]{1,0:T(1,128)S(1)}, f32[1,512]{1,0:T(1,128)S(1)}, u32[]{:S(2)}, u32[]{:S(2)}) collective-permute-start(f32[1,512]{1,0:T(1,128)S(1)} %collective-permute-done.13), channel_id=1, source_target_pairs={{0,4},{4,8},{8,12},{12,16},{16,20},{20,24},{24,28},{28,0},{1,5},{5... | collective-permute-start | bytes 6152 | tf_op jit(solution)/shard_map/ppermute | solution.py:13
  97.8 3.9 %collective-permute-start.17 = (f32[1,512]{1,0:T(1,128)S(1)}, f32[1,512]{1,0:T(1,128)S(1)}, u32[]{:S(2)}, u32[]{:S(2)}) collective-permute-start(f32[1,512]{1,0:T(1,128)S(1)} %collective-permute-done.16), channel_id=1, source_target_pairs={{0,28},{4,0},{8,4},{12,8},{16,12},{20,16},{24,20},{28,24},{1,29},{... | collective-permute-start | bytes 6152 | tf_op jit(solution)/shard_map/ppermute | solution.py:15
  102.9 8.8 %collective-permute-start.20 = (f32[768]{0:T(1024)S(1)}, f32[768]{0:T(1024)S(1)}, u32[]{:S(2)}, u32[]{:S(2)}) collective-permute-start(f32[768]{0:T(1024)S(1)} %fusion.72), channel_id=1, source_target_pairs={{0,3},{1,0},{2,1},{3,2},{4,7},{5,4},{6,5},{7,6},{8,11},{9,8},{10,9... | collective-permute-start | bytes 9224 | tf_op jit(solution)/shard_map/ppermute | solution.py:22
  106.3 6.5 %collective-permute-start.21 = (f32[768]{0:T(1024)S(1)}, f32[768]{0:T(1024)S(1)}, u32[]{:S(2)}, u32[]{:S(2)}) collective-permute-start(f32[768]{0:T(1024)S(1)} %fusion.72), channel_id=1, source_target_pairs={{0,2},{1,3},{2,0},{3,1},{4,6},{5,7},{6,4},{7,5},{8,10},{9,11},{10,... | collective-permute-start | bytes 9224 | tf_op jit(solution)/shard_map/ppermute | solution.py:22
  108.1 7.7 %collective-permute-start.18 = (f32[768]{0:T(1024)S(1)}, f32[768]{0:T(1024)S(1)}, u32[]{:S(2)}, u32[]{:S(2)}) collective-permute-start(f32[768]{0:T(1024)S(1)} %broadcast_multiply_fusion.2), channel_id=1, source_target_pairs={{0,1},{1,2},{2,3},{3,0},{4,5},{5,6},{6,7},{7,4},{8,9},{9,10},{10,1... | collective-permute-start | bytes 9224 | tf_op jit(solution)/shard_map/ppermute | solution.py:22
  109.9 5.9 %collective-permute-start.19 = (f32[768]{0:T(1024)S(1)}, f32[768]{0:T(1024)S(1)}, u32[]{:S(2)}, u32[]{:S(2)}) collective-permute-start(f32[768]{0:T(1024)S(1)} %broadcast_multiply_fusion), channel_id=1, source_target_pairs={{0,2},{1,3},{2,0},{3,1},{4,6},{5,7},{6,4},{7,5},{8,10},{9,11},{10,... | collective-permute-start | bytes 9224 | tf_op jit(solution)/shard_map/ppermute | solution.py:22
  (2 other events, 29.3 us)
Sparse Core Ops, SparseCore 0:
  43.8 41.0 reduce-scatter.6
  118.2 40.9 reduce-scatter.8
